TPU v7x, 32 devices: a whole 2x2x4 slice. The times are simulated.
32 devices in a mesh: rows: 4 (over y, x), cols: 8 (over z, core).
Axes of the slice: x: 2, y: 2, z: 4, core: 2. Of those that a mesh axis runs over, the one named last changes fastest.
Arguments:
- spectra: bfloat16 [1024, 4096], P(('rows', 'cols')), may hold values from -6 to 6
- band_weights: float32 [2048], replicated, may hold values from 0.3 to 3
- lag_weights: float32 [4], replicated, may hold values from 0.5 to 2
- selected_bins: int32 [8], replicated, may hold values from 0 to 7
Outputs:
- correlations: float32 [4, 1024, 1024], P(None, 'rows', 'cols')
- gradient: float32 [1024, 4096], P(('rows', 'cols'))
All inputs are finite; a program needn't handle non-finite values.
Results may differ from a plain program's by a relative error of at most 0.0045.
Values may be sent and summed in bfloat16 or wider, within the bound.
No kernel may reach another device: no remote copies, remote signals or barrier semaphores. Data moves between devices by JAX's collectives and lax.ppermute only.
A program may use at most 128 MiB of HBM per device.

v0:
```python
import jax
import jax.numpy as jnp
from jax import lax
from jax.sharding import PartitionSpec as P

LAGS = 4
LAG_STEP = 8
BIN = 128


def per_device(spectra, band_weights, lag_weights, selected_bins):
    n_rows = lax.axis_size("rows")
    n_cols = lax.axis_size("cols")
    row_index = lax.axis_index("rows")
    col_index = lax.axis_index("cols")
    freqs = band_weights.shape[0]
    raw = spectra.astype(jnp.float32)
    mean_power = jnp.mean(raw * raw, axis=1, keepdims=True)
    bin_gains = jnp.concatenate([band_weights, band_weights])
    whitened = (raw * lax.rsqrt(mean_power + 1e-05) * bin_gains[None, :]).astype(jnp.bfloat16)
    row_tile = lax.all_gather(whitened, "cols", axis=0, tiled=True)
    row_len = row_tile.shape[0]
    fold_ratio = n_cols // n_rows
    col_len = row_len // fold_ratio
    slot_part = col_index % fold_ratio
    owner_row = col_index // fold_ratio
    own_piece = lax.dynamic_slice_in_dim(row_tile, slot_part * col_len, col_len, 0)
    stacked = lax.all_gather(own_piece, "rows", axis=0, tiled=True)
    col_tile = lax.dynamic_slice_in_dim(stacked, owner_row * col_len, col_len, 0)
    row_chan = row_index * row_len + jnp.arange(row_len, dtype=jnp.int32)
    col_chan = col_index * col_len + jnp.arange(col_len, dtype=jnp.int32)
    distance = jnp.abs(row_chan[:, None] - col_chan[None, :]) // BIN
    selected = jnp.any(distance[:, :, None] == selected_bins[None, None, :], axis=2).astype(
        jnp.float32
    )
    norm_scale = 1.0 / jnp.sqrt(jnp.float32(2 * freqs))
    bin_index = jnp.arange(freqs, dtype=jnp.float32)
    real_part = row_tile[:, :freqs].astype(jnp.float32)
    imag_part = row_tile[:, freqs:].astype(jnp.float32)
    outputs = []
    row_grad = jnp.zeros((row_len, 2 * freqs), jnp.float32)
    col_grad = jnp.zeros((col_len, 2 * freqs), jnp.float32)
    for lag_index in range(LAGS):
        shift_lag = float((lag_index - LAGS // 2) * LAG_STEP)
        theta = jnp.pi * bin_index * shift_lag / freqs
        cosine = jnp.cos(theta)
        sine_part = jnp.sin(theta)
        rotated = jnp.concatenate(
            [
                real_part * cosine - imag_part * sine_part,
                imag_part * cosine + real_part * sine_part,
            ],
            axis=1,
        ).astype(jnp.bfloat16)
        correlation = (
            lax.dot_general(
                rotated, col_tile, (((1,), (1,)), ((), ())), preferred_element_type=jnp.float32
            )
            * norm_scale
        )
        outputs.append(correlation)
        adjoint = (lag_weights[lag_index] * selected * correlation).astype(jnp.bfloat16)
        back = jnp.dot(adjoint, col_tile, preferred_element_type=jnp.float32) * norm_scale
        back_real = back[:, :freqs]
        back_imag = back[:, freqs:]
        row_grad = row_grad + jnp.concatenate(
            [
                back_real * cosine + back_imag * sine_part,
                back_imag * cosine - back_real * sine_part,
            ],
            axis=1,
        )
        col_grad = (
            col_grad
            + lax.dot_general(
                adjoint, rotated, (((0,), (0,)), ((), ())), preferred_element_type=jnp.float32
            )
            * norm_scale
        )
    col_total = lax.psum(col_grad, "rows")
    is_owner = (owner_row == row_index).astype(jnp.float32)
    addition = lax.dynamic_update_slice_in_dim(
        jnp.zeros_like(row_grad), col_total * is_owner, slot_part * col_len, 0
    )
    gradient = lax.psum_scatter(row_grad + addition, "cols", scatter_dimension=0, tiled=True)
    return (jnp.stack(outputs), gradient)


def solution(mesh):
    placed = (P(("rows", "cols"), None), P(), P(), P())
    return jax.shard_map(
        per_device,
        mesh=mesh,
        in_specs=placed,
        out_specs=(P(None, "rows", "cols"), P(("rows", "cols"), None)),
        check_vma=False,
    )
```

profile of v0, /device:TPU:0, one launch (start us, length us, event | category | flops | bytes accessed | tf_op | source)
XLA Modules:
  0.0 241.0 jit_solution(7234839947374207454)
XLA Ops:
  7.2 0.0 all-gather.3.cloned.1.call-start
  7.2 0.8 pad_maximum_fusion.21
  8.0 0.0 copy-start.8
  8.0 1.1 fusion.28
  9.1 0.0 copy-start.9
  9.1 1.8 fusion.30
  10.9 0.0 all-gather.3.cloned.1.call-update
  10.9 0.0 all-gather.5.cloned.1.call-start
  11.0 32.0 %all-gather.3.cloned.1.call-done = bf16[256,4096]{1,0:T(8,128)(2,1)} async-done(((bf16[32,4096]{1,0:T(8,128)(2,1)}), bf16[256,4096]{1,0:T(8,128)(2,1)}) %all-gather.3.cloned.1.call-update) | async-done | bytes 2097168 | tf_op jit(solution)/shard_map/all_gather | solution.py:21
  43.0 0.0 copy-start
  43.0 2.4 %constant_dynamic-slice_fusion = bf16[128,4096]{1,0:T(8,128)(2,1)} fusion(bf16[256,4096]{1,0:T(8,128)(2,1)} %all-gather.3.cloned.1.call-done, s32[]{:T(128)S(6)} %select_n.28), kind=kLoop, calls=%fused_computation.115 | loop fusion | bytes 2097156 | tf_op jit(solution)/shard_map/dynamic_slice | solution.py:27
  45.4 0.0 all-gather.5.cloned.1.call-update
  45.5 0.0 all-reduce.2.cloned.1.call-start
  45.6 0.0 copy-done.8
  45.6 0.6 fusion.74
  46.2 0.1 fusion.42
  46.2 0.1 fusion.44
  46.3 0.1 fusion.48
  46.4 0.1 fusion.46
  46.4 0.2 add_select_fusion
  46.6 0.0 copy-done.9
  46.6 0.4 compare_reduce_fusion
  47.0 0.0 copy-done
  47.0 1.6 fusion.8
  48.7 3.4 %fusion.4 = (bf16[256,2048]{1,0:T(8,128)(2,1)}, bf16[256,2048]{1,0:T(8,128)(2,1)}, bf16[256,2048]{1,0:T(8,128)(2,1)}, bf16[256,2048]{1,0:T(8,128)(2,1)}, bf16[25...) fusion(f32[2048]{0:T(1024)S(1)} %get-tuple-element.30, f32[2048]{0:T(1024)S(1)} %get-tuple-element.31, ...), kind=kLoop, calls=%fused_computation.28 | loop fusion | flops 13631488 | bytes 8437760 | tf_op jit(solution)/shard_map/convert.6
  52.1 45.5 %all-gather.5.cloned.1.call-done = bf16[512,4096]{1,0:T(8,128)(2,1)} async-done(((bf16[128,4096]{1,0:T(8,128)(2,1)}), bf16[512,4096]{1,0:T(8,128)(2,1)}) %all-gather.5.cloned.1.call-update) | async-done | bytes 4194320 | tf_op jit(solution)/shard_map/all_gather | solution.py:28
  97.6 0.0 copy-start.2
  97.6 2.7 %fusion.24 = f32[256,128]{1,0:T(8,128)S(1)} fusion(bf16[256,2048]{1,0:T(8,128)(2,1)} %get-tuple-element.11, bf16[256,2048]{1,0:T(8,128)(2,1)} %get-tuple-element.10, bf16[512,4096]{1,0:T(8,128)(2,1)} %all-gather.5.cloned.1.call-done, s32[]{:T(128)S(6)} %select_n.30), kind=kOutput, calls=%fused_computation.61 | convolution fusion | flops 272662528 | bytes 3276804 | tf_op jit(solution)/shard_map/dot_general | solution.py:56
  100.3 0.0 copy-start.1
  100.3 2.7 %fusion.22 = f32[128,4096]{1,0:T(8,128)S(1)} fusion(bf16[256,2048]{1,0:T(8,128)(2,1)} %get-tuple-element.11, bf16[256,2048]{1,0:T(8,128)(2,1)} %get-tuple-element.10, f32[256,128]{1,0:T(8,128)S(1)} %fusion.24, pred[256,128]{1,0:T(8,128)(4,1)S(1)} %compare_reduce_fusion, f32[]{:T(128)} %bitcast.4), kind=kOutput, calls=%fused_computation.59 | convolution fusion | flops 272728064 | bytes 4358148 | tf_op jit(solution)/shard_map/dot_general | solution.py:75
  103.0 0.0 copy-done.2
  103.0 0.0 copy-done.1
  103.0 0.7 fusion.25
  103.8 0.0 copy-start.6
  103.8 0.0 copy-start.7
  103.8 1.3 convolution_add_fusion.2
  105.1 0.0 copy-done.6
  105.1 0.2 copy-done.7
  105.3 0.7 fusion.26
  106.0 0.0 copy-start.4
  106.0 0.0 copy-start.5
  106.0 1.3 convolution_add_fusion.1
  107.3 0.0 copy-done.4
  107.3 0.3 copy-done.5
  107.6 0.7 fusion.27
  108.3 2.5 %fusion = f32[128,4096]{1,0:T(8,128)} fusion(f32[128,4096]{1,0:T(8,128)S(1)} %convolution_add_fusion.1, bf16[256,2048]{1,0:T(8,128)(2,1)S(1)} %copy-done.4, bf16[256,2048]{1,0:T(8,128)(2,1)S(1)} %copy-done.5, f32[256,128]{1,0:T(8,128)S(1)} %fusion.27, pred[256,128]{1,0:T(8,128)(4,1)S(1)} %compare_reduce_fusion, f32[]{:T(128)} %bitcast.7), kind=kOutput, calls=%fused_computation.21 | convolution fusion | flops 273776640 | bytes 6455300 | tf_op jit(solution)/shard_map/dot_general | solution.py:75
  110.8 0.0 all-reduce.2.cloned.1.call-update
  110.9 0.2 reduce-scatter.2.cloned.1.call-start
  111.1 2.5 %convolution_multiply_fusion.3 = f32[256,4096]{1,0:T(8,128)S(1)} fusion(bf16[512,4096]{1,0:T(8,128)(2,1)} %all-gather.5.cloned.1.call-done, s32[]{:T(128)S(6)} %select_n.30, f32[256,128]{1,0:T(8,128)S(1)} %fusion.24, pred[256,128]{1,0:T(8,128)(4,1)S(1)} %compare_reduce_fusion, f32[]{:T(128)} %bitcast.4), kind=kOutput, calls=%fused_computation.19 | convolution fusion | flops 269582336 | bytes 5407236 | tf_op jit(solution)/shard_map/dot_general | solution.py:63
  113.6 0.0 copy-start.3
  113.6 0.6 multiply_add_fusion.3
  114.2 1.6 copy-done.3
  115.8 1.3 convolution_multiply_fusion.1
  117.1 0.6 multiply_add_fusion.1
  117.7 1.3 convolution_multiply_fusion
  119.1 1.3 convolution_multiply_fusion.2
  120.4 0.6 multiply_add_fusion
  121.0 0.6 multiply_add_fusion.2
  121.6 2.5 %fusion.2 = f32[256,4096]{1,0:T(8,128)} fusion(f32[256,2048]{1,0:T(8,128)S(1)} %get-tuple-element.9, f32[256,2048]{1,0:T(8,128)S(1)} %get-tuple-element.8, f32[256,2048]{1,0:T(8,128)S(1)} %get-tuple-element.7, f32[256,2048]{1,0:T(8,128)S(1)} %get-tuple-element.6, f32[256,2048]{1,0:T(8,128)S(1)} %get-tuple-element.5, f32[256,2048]{1,0:T(8,128)S(1)} %get-tuple-element.4, ...), kind=kLoop, calls=%fused_computation.26 | loop fusion | flops 7340032 | bytes 20971520 | tf_op jit(solution)/shard_map/add | solution.py:66
  124.2 56.3 %all-reduce.2.cloned.1.call-done = f32[128,4096]{1,0:T(8,128)} async-done(((f32[128,4096]{1,0:T(8,128)}), f32[128,4096]{1,0:T(8,128)}) %all-reduce.2.cloned.1.call-update) | async-done | bytes 2097168 | tf_op jit(solution)/shard_map/psum | solution.py:80
  180.5 3.8 %add_dynamic-update-slice_fusion = f32[256,4096]{1,0:T(8,128)} fusion(f32[256,4096]{1,0:T(8,128)} %fusion.2, s32[]{:T(128)S(6)} %select_n.28, f32[128,4096]{1,0:T(8,128)} %all-reduce.2.cloned.1.call-done, f32[]{:T(128)S(6)} %convert_element_type.40), kind=kLoop, calls=%fused_computation.47 | loop fusion | flops 1048576 | bytes 6291464 | tf_op jit(solution)/shard_map/add | solution.py:85
  184.3 0.0 reduce-scatter.2.cloned.1.call-update
  184.3 0.8 pad_maximum_fusion.20
  185.2 49.3 %reduce-scatter.2.cloned.1.call-done = f32[32,4096]{1,0:T(8,128)} async-done(((f32[256,4096]{1,0:T(8,128)}), f32[32,4096]{1,0:T(8,128)}) %reduce-scatter.2.cloned.1.call-update) | async-done | bytes 524304 | tf_op jit(solution)/shard_map/reduce_scatter | solution.py:85
  (3 shorter events, 0.0 us)
Async XLA Ops:
  7.2 35.8 %all-gather.3.cloned.1.call-start = ((), (), s32[]{:S(2)}) async-start(), calls=%async_computation.1 | async-start | bytes 2359296 | tf_op jit(solution)/shard_map/all_gather | solution.py:21
  8.0 37.6 %copy-start.8 = (f32[4]{0:T(128)S(1)}, f32[4]{0:T(128)}, u32[]{:S(2)}) copy-start(f32[4]{0:T(128)} %param.6) | copy-start | bytes 52
  9.1 37.5 %copy-start.9 = (s32[8]{0:T(128)S(1)}, s32[8]{0:T(128)}, u32[]{:S(2)}) copy-start(s32[8]{0:T(128)} %param.7) | copy-start | bytes 100
  10.9 86.6 %all-gather.5.cloned.1.call-start = ((), (), s32[]{:S(2)}) async-start(), calls=%async_computation.2 | async-start | bytes 5242880 | tf_op jit(solution)/shard_map/all_gather | solution.py:28
  43.0 4.0 %copy-start = (bf16[256,4096]{1,0:T(8,128)(2,1)S(1)}, bf16[256,4096]{1,0:T(8,128)(2,1)}, u32[]{:S(2)}) copy-start(bf16[256,4096]{1,0:T(8,128)(2,1)} %all-gather.3.cloned.1.call-done) | copy-start | bytes 6291460
  45.5 135.0 %all-reduce.2.cloned.1.call-start = ((), (), s32[]{:S(2)}) async-start(), calls=%async_computation.3 | async-start | bytes 4194304 | tf_op jit(solution)/shard_map/psum | solution.py:80
  97.6 5.4 %copy-start.2 = (bf16[512,4096]{1,0:T(8,128)(2,1)S(1)}, bf16[512,4096]{1,0:T(8,128)(2,1)}, u32[]{:S(2)}) copy-start(bf16[512,4096]{1,0:T(8,128)(2,1)} %all-gather.5.cloned.1.call-done) | copy-start | bytes 12582916
  100.3 2.7 %copy-start.1 = (bf16[256,2048]{1,0:T(8,128)(2,1)S(1)}, bf16[256,2048]{1,0:T(8,128)(2,1)}, u32[]{:S(2)}) copy-start(bf16[256,2048]{1,0:T(8,128)(2,1)} %get-tuple-element.13) | copy-start | bytes 3145732
  103.8 1.3 copy-start.6
  103.8 1.5 copy-start.7
  106.0 1.3 copy-start.4
  106.0 1.5 copy-start.5
  110.9 123.6 %reduce-scatter.2.cloned.1.call-start = ((), (), s32[]{:S(2)}) async-start(), calls=%async_computation.4 | async-start | bytes 4718592 | tf_op jit(solution)/shard_map/reduce_scatter | solution.py:85
  113.6 2.2 copy-start.3
Sparse Core Ops, SparseCore 0:
  11.1 31.8 all-gather.2
  45.6 51.9 all-gather.4
  111.0 69.4 all-reduce.1
  184.5 49.9 reduce-scatter.1
where the time goes:
time: 241 us
  waiting for transfers between devices  183 us (76%)
  matrix products  19.2 us (8%)
  other arithmetic  19.1 us (8%)
  between operations  14.1 us (6%)
  local copies, waits for them, and re-layouts  5.18 us (2%)
    psum x1, waiting for transfers between devices, per_device(): col_total = lax.psum(col_grad, 'rows')  56.3 us
    reduce_scatter x1, waiting for transfers between devices, per_device(): lax.psum_scatter(row_grad + addition, 'cols', scatter_dimension=0, tiled=...  49.3 us
    all_gather x1, waiting for transfers between devices, per_device(): stacked = lax.all_gather(own_piece, 'rows', axis=0, tiled=True)  45.5 us
    all_gather x1, waiting for transfers between devices, per_device(): row_tile = lax.all_gather(whitened, 'cols', axis=0, tiled=True)  32 us
    dot_general x4, matrix products, per_device(): lax.dot_general(adjoint, rotated, (((0,), (0,)), ((), ())), preferred_ele...  7.8 us
    dot_general x4, matrix products, per_device(): jnp.dot(adjoint, col_tile, preferred_element_type=jnp.float32) * norm_scale  6.53 us
    another operation x2, other arithmetic  5.08 us
    dot_general x4, matrix products, per_device(): lax.dot_general(rotated, col_tile, (((1,), (1,)), ((), ())), preferred_el...  4.84 us
  transfers between devices with their start and end apart: 4, of which 4 were waited for; matrix products, arithmetic and copies ran while one was open for 8% of the time, Pallas kernels for 0%

commit v1 on v0

--- a/solution.py
+++ b/solution.py
@@ -77,7 +77,11 @@
             )
             * norm_scale
         )
-    col_total = lax.psum(col_grad, "rows")
+    col_total = col_grad
+    for hop in (1, 2):
+        col_total = col_total + lax.ppermute(
+            col_total, "rows", [(dev, dev ^ hop) for dev in range(4)]
+        )
     is_owner = (owner_row == row_index).astype(jnp.float32)
     addition = lax.dynamic_update_slice_in_dim(
         jnp.zeros_like(row_grad), col_total * is_owner, slot_part * col_len, 0

time: 241 us -> 264 us (1.095)
  waiting for transfers between devices: 183 us -> 206 us
  starting transfers between devices: 0.35 us -> 3.18 us
    ppermute x0 -> x2, waiting for transfers between devices: none -> 79.6 us  [per_device(): lax.ppermute(col_total, 'rows', [(dev, dev ^ hop) for dev in range(4)])]
    psum x1 -> x0, waiting for transfers between devices: 56.3 us -> none  [per_device(): col_total = lax.psum(col_grad, 'rows')]
    ppermute x0 -> x2, starting transfers between devices: none -> 3.05 us  [per_device(): lax.ppermute(col_total, 'rows', [(dev, dev ^ hop) for dev in range(4)])]
  transfers between devices with their start and end apart: 4 -> 5, of which waited for: 4 -> 5; matrix products, arithmetic and copies ran while one was open for 8% -> 7% of each run, Pallas kernels for 0% -> 0%
where the time goes in v1:
time: 264 us; the launch traced here: 263 us
  waiting for transfers between devices  206 us (78%)
  other arithmetic  19.6 us (7%)
  matrix products  16.7 us (6%)
  between operations  14.1 us (5%)
  local copies, waits for them, and re-layouts  3.54 us (1%)
  starting transfers between devices  3.18 us (1%)
    ppermute x2, waiting for transfers between devices, per_device(): lax.ppermute(col_total, 'rows', [(dev, dev ^ hop) for dev in range(4)])  79.6 us
    reduce_scatter x1, waiting for transfers between devices, per_device(): lax.psum_scatter(row_grad + addition, 'cols', scatter_dimension=0, tiled=...  49.2 us
    all_gather x1, waiting for transfers between devices, per_device(): stacked = lax.all_gather(own_piece, 'rows', axis=0, tiled=True)  45.5 us
    all_gather x1, waiting for transfers between devices, per_device(): row_tile = lax.all_gather(whitened, 'cols', axis=0, tiled=True)  32 us
    dot_general x4, matrix products, per_device(): lax.dot_general(adjoint, rotated, (((0,), (0,)), ((), ())), preferred_ele...  6.51 us
    dot_general x4, matrix products, per_device(): jnp.dot(adjoint, col_tile, preferred_element_type=jnp.float32) * norm_scale  5.35 us
  transfers between devices with their start and end apart: 5, of which 5 were waited for; matrix products, arithmetic and copies ran while one was open for 7% of the time, Pallas kernels for 0%

profile of v1, /device:TPU:0, one launch (start us, length us, event | category | flops | bytes accessed | tf_op | source)
XLA Modules:
  0.0 263.3 jit_solution(4525904763638092327)
XLA Ops:
  7.2 0.0 all-gather.3.cloned.1.call-start
  7.2 0.8 pad_maximum_fusion.21
  8.0 0.0 copy-start.7
  8.0 1.1 fusion.28
  9.1 0.0 copy-start.8
  9.1 1.8 fusion.30
  10.9 0.0 all-gather.3.cloned.1.call-update
  10.9 0.0 all-gather.5.cloned.1.call-start
  11.0 32.0 %all-gather.3.cloned.1.call-done = bf16[256,4096]{1,0:T(8,128)(2,1)} async-done(((bf16[32,4096]{1,0:T(8,128)(2,1)}), bf16[256,4096]{1,0:T(8,128)(2,1)}) %all-gather.3.cloned.1.call-update) | async-done | bytes 2097168 | tf_op jit(solution)/shard_map/all_gather | solution.py:21
  43.0 0.0 copy-start
  43.0 2.4 constant_dynamic-slice_fusion
  45.4 0.0 all-gather.5.cloned.1.call-update
  45.4 0.0 reduce-scatter.2.cloned.1.call-start
  45.6 0.0 copy-done.7
  45.6 0.7 fusion.74
  46.2 0.1 fusion.42
  46.3 0.1 fusion.44
  46.3 0.1 fusion.48
  46.4 0.1 fusion.46
  46.4 0.2 add_select_fusion
  46.6 0.0 copy-done.8
  46.6 0.4 compare_reduce_fusion
  47.0 0.0 copy-done
  47.0 1.7 fusion.8
  48.7 3.4 %fusion.4 = (bf16[256,2048]{1,0:T(8,128)(2,1)}, bf16[256,2048]{1,0:T(8,128)(2,1)}, bf16[256,2048]{1,0:T(8,128)(2,1)}, bf16[256,2048]{1,0:T(8,128)(2,1)}, bf16[25...) fusion(f32[2048]{0:T(1024)S(1)} %get-tuple-element.30, f32[2048]{0:T(1024)S(1)} %get-tuple-element.31, ...), kind=kLoop, calls=%fused_computation.28 | loop fusion | flops 13631488 | bytes 8437760 | tf_op jit(solution)/shard_map/convert.6
  52.1 45.5 %all-gather.5.cloned.1.call-done = bf16[512,4096]{1,0:T(8,128)(2,1)} async-done(((bf16[128,4096]{1,0:T(8,128)(2,1)}), bf16[512,4096]{1,0:T(8,128)(2,1)}) %all-gather.5.cloned.1.call-update) | async-done | bytes 4194320 | tf_op jit(solution)/shard_map/all_gather | solution.py:28
  97.6 0.0 copy-start.2
  97.6 2.7 %fusion.24 = f32[256,128]{1,0:T(8,128)S(1)} fusion(bf16[256,2048]{1,0:T(8,128)(2,1)} %get-tuple-element.11, bf16[256,2048]{1,0:T(8,128)(2,1)} %get-tuple-element.10, bf16[512,4096]{1,0:T(8,128)(2,1)} %all-gather.5.cloned.1.call-done, s32[]{:T(128)S(6)} %select_n.30), kind=kOutput, calls=%fused_computation.61 | convolution fusion | flops 272662528 | bytes 3276804 | tf_op jit(solution)/shard_map/dot_general | solution.py:56
  100.3 0.0 copy-start.1
  100.3 2.7 %fusion.22 = f32[128,4096]{1,0:T(8,128)S(1)} fusion(bf16[256,2048]{1,0:T(8,128)(2,1)} %get-tuple-element.11, bf16[256,2048]{1,0:T(8,128)(2,1)} %get-tuple-element.10, f32[256,128]{1,0:T(8,128)S(1)} %fusion.24, pred[256,128]{1,0:T(8,128)(4,1)S(1)} %compare_reduce_fusion, f32[]{:T(128)} %bitcast.4), kind=kOutput, calls=%fused_computation.59 | convolution fusion | flops 272728064 | bytes 4358148 | tf_op jit(solution)/shard_map/dot_general | solution.py:75
  103.0 0.0 copy-done.2
  103.0 0.0 copy-done.1
  103.0 0.7 fusion.25
  103.8 0.0 copy-start.5
  103.8 0.0 copy-start.6
  103.8 1.3 convolution_add_fusion.2
  105.1 0.0 copy-done.5
  105.1 0.2 copy-done.6
  105.3 0.7 fusion.26
  106.0 0.0 copy-start.3
  106.0 0.0 copy-start.4
  106.0 1.3 convolution_add_fusion.1
  107.4 0.0 copy-done.3
  107.4 0.2 copy-done.4
  107.6 0.7 fusion.27
  108.3 1.2 fusion
  109.5 1.5 collective-permute-start
  111.0 1.3 convolution_multiply_fusion.3
  112.3 1.4 convolution_multiply_fusion.1
  113.7 1.3 convolution_multiply_fusion
  115.0 0.8 multiply_add_fusion.3
  115.9 0.9 multiply_add_fusion.1
  116.8 40.0 %collective-permute-done = f32[128,4096]{1,0:T(8,128)S(1)} collective-permute-done((f32[128,4096]{1,0:T(8,128)S(1)}, f32[128,4096]{1,0:T(8,128)S(1)}, u32[]{:S(2)}, u32[]{:S(2)}) %collective-permute-start) | collective-permute-done | bytes 2097184 | tf_op jit(solution)/shard_map/ppermute | solution.py:82
  156.8 0.2 add.131
  157.0 1.5 collective-permute-start.1
  158.5 1.3 convolution_multiply_fusion.2
  159.9 0.6 multiply_add_fusion
  160.5 0.8 multiply_add_fusion.2
  161.3 2.5 fusion.2
  163.8 39.6 %collective-permute-done.1 = f32[128,4096]{1,0:T(8,128)S(1)} collective-permute-done((f32[128,4096]{1,0:T(8,128)S(1)}, f32[128,4096]{1,0:T(8,128)S(1)}, u32[]{:S(2)}, u32[]{:S(2)}) %collective-permute-start.1) | collective-permute-done | bytes 2097184 | tf_op jit(solution)/shard_map/ppermute | solution.py:82
  203.4 3.3 %add_dynamic-update-slice_fusion = f32[256,4096]{1,0:T(8,128)} fusion(f32[256,4096]{1,0:T(8,128)} %fusion.2, s32[]{:T(128)S(6)} %select_n.28, f32[128,4096]{1,0:T(8,128)S(1)} %add.131, f32[128,4096]{1,0:T(8,128)S(1)} %collective-permute-done.1, f32[]{:T(128)S(6)} %convert_element_type.40), kind=kLoop, calls=%fused_computation.47 | loop fusion | flops 1572864 | bytes 8388616 | tf_op jit(solution)/shard_map/add | solution.py:89
  206.7 0.0 reduce-scatter.2.cloned.1.call-update
  206.8 0.8 pad_maximum_fusion.20
  207.6 49.2 %reduce-scatter.2.cloned.1.call-done = f32[32,4096]{1,0:T(8,128)} async-done(((f32[256,4096]{1,0:T(8,128)}), f32[32,4096]{1,0:T(8,128)}) %reduce-scatter.2.cloned.1.call-update) | async-done | bytes 524304 | tf_op jit(solution)/shard_map/reduce_scatter | solution.py:89
  (3 shorter events, 0.0 us)
Async XLA Ops:
  7.2 35.8 %all-gather.3.cloned.1.call-start = ((), (), s32[]{:S(2)}) async-start(), calls=%async_computation.1 | async-start | bytes 2359296 | tf_op jit(solution)/shard_map/all_gather | solution.py:21
  8.0 37.6 %copy-start.7 = (f32[4]{0:T(128)S(1)}, f32[4]{0:T(128)}, u32[]{:S(2)}) copy-start(f32[4]{0:T(128)} %param.6) | copy-start | bytes 52
  9.1 37.5 %copy-start.8 = (s32[8]{0:T(128)S(1)}, s32[8]{0:T(128)}, u32[]{:S(2)}) copy-start(s32[8]{0:T(128)} %param.7) | copy-start | bytes 100
  10.9 86.6 %all-gather.5.cloned.1.call-start = ((), (), s32[]{:S(2)}) async-start(), calls=%async_computation.2 | async-start | bytes 5242880 | tf_op jit(solution)/shard_map/all_gather | solution.py:28
  43.0 4.1 %copy-start = (bf16[256,4096]{1,0:T(8,128)(2,1)S(1)}, bf16[256,4096]{1,0:T(8,128)(2,1)}, u32[]{:S(2)}) copy-start(bf16[256,4096]{1,0:T(8,128)(2,1)} %all-gather.3.cloned.1.call-done) | copy-start | bytes 6291460
  45.4 211.4 %reduce-scatter.2.cloned.1.call-start = ((), (), s32[]{:S(2)}) async-start(), calls=%async_computation.3 | async-start | bytes 4718592 | tf_op jit(solution)/shard_map/reduce_scatter | solution.py:89
  97.6 5.4 %copy-start.2 = (bf16[512,4096]{1,0:T(8,128)(2,1)S(1)}, bf16[512,4096]{1,0:T(8,128)(2,1)}, u32[]{:S(2)}) copy-start(bf16[512,4096]{1,0:T(8,128)(2,1)} %all-gather.5.cloned.1.call-done) | copy-start | bytes 12582916
  100.3 2.7 %copy-start.1 = (bf16[256,2048]{1,0:T(8,128)(2,1)S(1)}, bf16[256,2048]{1,0:T(8,128)(2,1)}, u32[]{:S(2)}) copy-start(bf16[256,2048]{1,0:T(8,128)(2,1)} %get-tuple-element.13) | copy-start | bytes 3145732
  103.8 1.3 copy-start.5
  103.8 1.5 copy-start.6
  106.0 1.4 copy-start.3
  106.0 1.5 copy-start.4
  109.5 47.3 %collective-permute-start = (f32[128,4096]{1,0:T(8,128)S(1)}, f32[128,4096]{1,0:T(8,128)S(1)}, u32[]{:S(2)}, u32[]{:S(2)}) collective-permute-start(f32[128,4096]{1,0:T(8,128)S(1)} %fusion), channel_id=1, source_target_pairs={{0,8},{8,0},{16,24},{24,16},{1,9},{9,1},{17,25},{25,17},{2,10},{10... | collective-permute-start | bytes 6291464 | tf_op jit(solution)/shard_map/ppermute | solution.py:82
  157.0 46.4 %collective-permute-start.1 = (f32[128,4096]{1,0:T(8,128)S(1)}, f32[128,4096]{1,0:T(8,128)S(1)}, u32[]{:S(2)}, u32[]{:S(2)}) collective-permute-start(f32[128,4096]{1,0:T(8,128)S(1)} %add.131), channel_id=1, source_target_pairs={{0,16},{8,24},{16,0},{24,8},{1,17},{9,25},{17,1},{25,9},{2,18},{10... | collective-permute-start | bytes 6291464 | tf_op jit(solution)/shard_map/ppermute | solution.py:82
Sparse Core Ops, SparseCore 0:
  11.1 31.8 all-gather.2
  45.6 51.9 all-gather.4
  206.9 49.8 reduce-scatter.1
